TPU v7x, 128 devices: a whole 4x4x4 slice. The times are simulated.
128 devices in a mesh: dp: 16 (over x, z), fsdp: 8 (over y, core).
Axes of the slice: x: 4, y: 4, z: 4, core: 2. Of those that a mesh axis runs over, the one named last changes fastest.
Arguments:
- inputs: float32 [49152, 768], P(('dp', 'fsdp'))
- encoded: bfloat16 [24576, 768], P(('dp', 'fsdp'))
- cotangent: float32 [49152, 768], P(('dp', 'fsdp')), may hold values from -6 to 6
- scoring: bfloat16 [3072, 768], P(('dp', 'fsdp'))
- weights: bfloat16 [9216, 768], P(('dp', 'fsdp'))
- small_params: bfloat16 [2688], P(('dp', 'fsdp'))
- dec_segments: int32 [128, 384], P(('dp', 'fsdp')), may hold values from 0 to 5, as said below
- enc_segments: int32 [128, 192], P(('dp', 'fsdp')), may hold values from 0 to 5, as said below
Outputs:
- output: float32 [49152, 768], P(('dp', 'fsdp'))
- grad_inputs: float32 [49152, 768], P(('dp', 'fsdp'))
- grad_encoded: float32 [24576, 768], P(('dp', 'fsdp'))
- grad_scoring: float32 [3072, 768], P(('dp', 'fsdp'))
- grad_weights: float32 [9216, 768], P(('dp', 'fsdp'))
- grad_small: float32 [2688], P(('dp', 'fsdp'))
Inputs may be any that keep to these rules, and one draw needn't show every extreme that they name: In each row of dec_segments the ids start at 0, never fall, rise by at most 1 from one position to the next and change only at multiples of 64; group 0 holds one sequence of 384 rows. Row g of enc_segments is row g of dec_segments with each block of 64 equal ids shortened to 32 of them: encoder sequence s belongs to decoder sequence s of the same group.
All inputs are finite; a program needn't handle non-finite values.
Results may differ from a plain program's by a relative error of at most 0.025.
Values may be sent and summed in bfloat16 or wider, within the bound.
A program may use at most 192 MiB of HBM per device.

v0:
```python
import jax
import jax.numpy as jnp
import numpy as np
from jax import lax
from jax.sharding import PartitionSpec as P

D = 768
H = 12
DH = 64
FF = 2048
BUCKETS = 32


BUCKET_EDGES = [
    int(edge_value) for edge_value in np.ceil(16.0 * 8.0 ** ((np.arange(17, 32) - 16) / 16.0))
]
EPSILON = 1e-06
MASKED_SCORE = -1e30


def bucket_index(distance):
    distance = jnp.maximum(distance, 0)
    far_part = jnp.zeros_like(distance)
    for edge_value in BUCKET_EDGES:
        far_part = far_part + (distance >= edge_value).astype(distance.dtype)
    return jnp.where(distance < 16, distance, 16 + far_part).astype(jnp.int32)


def rms_scale(values, gain):
    mean_square = jnp.mean(values * values, axis=-1, keepdims=True)
    return values * lax.rsqrt(mean_square + EPSILON) * gain


def gelu_tanh(values):
    return jax.nn.gelu(values, approximate=True)


def to_half(values):
    return values.astype(jnp.bfloat16)


def dot_plain(left, right):
    return jnp.dot(left, right, preferred_element_type=jnp.float32)


def dot_rows(left, right):
    return lax.dot_general(
        left, right, (((0,), (0,)), ((), ())), preferred_element_type=jnp.float32
    )


def dot_cols(left, right):
    return lax.dot_general(
        left, right, (((1,), (1,)), ((), ())), preferred_element_type=jnp.float32
    )


def unpack(full_scoring, full_weights, full_small):
    score_parts = [full_scoring[index * D : (index + 1) * D] for index in range(4)]
    other_parts = [full_weights[index * D : (index + 1) * D] for index in range(4)]
    blocks = [
        score_parts[0],
        score_parts[1],
        other_parts[0],
        other_parts[1],
        score_parts[2],
        score_parts[3],
        other_parts[2],
        other_parts[3],
    ]
    ffn_base = 4 * D
    gate_rows = full_weights[ffn_base : ffn_base + FF]
    up_rows = full_weights[ffn_base + FF : ffn_base + 2 * FF]
    down_rows = full_weights[ffn_base + 2 * FF : ffn_base + 3 * FF]
    gains = full_small[: 3 * D].astype(jnp.float32).reshape(3, D)
    table = full_small[3 * D :].astype(jnp.float32).reshape(BUCKETS, H)
    return (blocks, gate_rows, up_rows, down_rows, gains, table)


def position_bias(buckets, table):
    total_bias = jnp.zeros((H,) + buckets.shape, jnp.float32)
    for bucket in range(BUCKETS):
        total_bias = total_bias + jnp.where(buckets == bucket, table[bucket][:, None, None], 0.0)
    return total_bias


def key_blocks(keys, values, key_seg):
    key_total = keys.shape[0]
    block_rows = 128 if key_total % 128 == 0 else 64
    block_total = key_total // block_rows
    return (
        keys.reshape(block_total, block_rows, H, DH),
        values.reshape(block_total, block_rows, H, DH),
        key_seg.reshape(block_total, block_rows),
        jnp.arange(block_total, dtype=jnp.int32) * block_rows,
    )


def block_scores(query_heads, key_block, block_seg, block_start, own_seg, query_rows, table):
    scores = jnp.einsum("khd,qhd->hkq", key_block, query_heads, preferred_element_type=jnp.float32)
    allowed = block_seg[:, None] == own_seg[None, :]
    buckets = None
    if table is not None:
        key_rows = block_start + jnp.arange(key_block.shape[0], dtype=jnp.int32)
        distance = query_rows[None, :] - key_rows[:, None]
        allowed = allowed & (distance >= 0)
        buckets = bucket_index(distance)
        scores = scores + position_bias(buckets, table)
    return (jnp.where(allowed[None], scores, MASKED_SCORE), allowed, buckets)


def attend_forward(queries, keys, values, key_seg, own_seg, query_rows, table):
    row_count = queries.shape[0]
    query_heads = queries.reshape(row_count, H, DH)
    pieces = key_blocks(keys, values, key_seg)

    def first_pass(carry, piece):
        row_max, row_total = carry
        key_block, _, block_seg, block_start = piece
        scores, _, _ = block_scores(
            query_heads, key_block, block_seg, block_start, own_seg, query_rows, table
        )
        new_max = jnp.maximum(row_max, jnp.max(scores, axis=1))
        row_total = row_total * jnp.exp(row_max - new_max) + jnp.sum(
            jnp.exp(scores - new_max[:, None, :]), axis=1
        )
        return ((new_max, row_total), None)

    start_max = jnp.full((H, row_count), MASKED_SCORE, jnp.float32)
    start_total = jnp.zeros((H, row_count), jnp.float32)
    (row_max, row_total), _ = lax.scan(first_pass, (start_max, start_total), pieces)
    log_total = row_max + jnp.log(row_total)

    def second_pass(context, piece):
        key_block, value_block, block_seg, block_start = piece
        scores, allowed, _ = block_scores(
            query_heads, key_block, block_seg, block_start, own_seg, query_rows, table
        )
        probs = jnp.where(allowed[None], jnp.exp(scores - log_total[:, None, :]), 0.0)
        context = context + jnp.einsum(
            "hkq,khd->qhd", to_half(probs), value_block, preferred_element_type=jnp.float32
        )
        return (context, None)

    context, _ = lax.scan(second_pass, jnp.zeros((row_count, H, DH), jnp.float32), pieces)
    return (to_half(context.reshape(row_count, D)), log_total)


def attend_backward(
    queries, keys, values, key_seg, own_seg, query_rows, table, log_total, context, grad_context
):
    row_count = queries.shape[0]
    query_heads = queries.reshape(row_count, H, DH)
    grad_heads = grad_context.reshape(row_count, H, DH)
    delta_rows = jnp.sum(
        grad_heads.astype(jnp.float32) * context.reshape(row_count, H, DH).astype(jnp.float32),
        axis=-1,
    ).T
    pieces = key_blocks(keys, values, key_seg)

    def one_block(carry, piece):
        grad_queries, grad_table = carry
        key_block, value_block, block_seg, block_start = piece
        scores, allowed, buckets = block_scores(
            query_heads, key_block, block_seg, block_start, own_seg, query_rows, table
        )
        probs = jnp.where(allowed[None], jnp.exp(scores - log_total[:, None, :]), 0.0)
        grad_values = jnp.einsum(
            "hkq,qhd->khd", to_half(probs), grad_heads, preferred_element_type=jnp.float32
        )
        grad_probs = jnp.einsum(
            "khd,qhd->hkq", value_block, grad_heads, preferred_element_type=jnp.float32
        )
        grad_scores = probs * (grad_probs - delta_rows[:, None, :])
        scaled = to_half(grad_scores)
        grad_queries = grad_queries + jnp.einsum(
            "hkq,khd->qhd", scaled, key_block, preferred_element_type=jnp.float32
        )
        grad_keys = jnp.einsum(
            "hkq,qhd->khd", scaled, query_heads, preferred_element_type=jnp.float32
        )
        if table is not None:
            one_hot = (buckets[..., None] == jnp.arange(BUCKETS, dtype=jnp.int32)).astype(
                jnp.float32
            )
            grad_table = grad_table + jnp.einsum(
                "hkq,kqb->bh", grad_scores, one_hot, precision=lax.Precision.HIGHEST
            )
        return ((grad_queries, grad_table), (grad_keys, grad_values))

    start = (jnp.zeros((row_count, H, DH), jnp.float32), jnp.zeros((BUCKETS, H), jnp.float32))
    (grad_queries, grad_table), (grad_keys, grad_values) = lax.scan(one_block, start, pieces)
    key_total = keys.shape[0]
    return (
        grad_queries.reshape(row_count, D),
        grad_keys.reshape(key_total, D),
        grad_values.reshape(key_total, D),
        grad_table,
    )


def per_device(
    inputs, encoded, cotangent, scoring, weights, small_params, dec_segments, enc_segments
):
    full_scoring, full_weights, full_small = (
        lax.all_gather(scoring, ("dp", "fsdp"), axis=0, tiled=True),
        lax.all_gather(weights, ("dp", "fsdp"), axis=0, tiled=True),
        lax.all_gather(small_params, ("dp", "fsdp"), axis=0, tiled=True),
    )
    blocks, gate_rows, up_rows, down_rows, gains, table = unpack(
        full_scoring, full_weights, full_small
    )
    row_count = inputs.shape[0]
    query_rows = jnp.arange(row_count, dtype=jnp.int32)
    own_seg = dec_segments[0]
    enc_seg = enc_segments[0]
    normed_one = to_half(rms_scale(inputs, gains[0]))
    self_queries = to_half(dot_plain(normed_one, blocks[0]))
    self_keys = to_half(dot_plain(normed_one, blocks[1]))
    self_values = to_half(dot_plain(normed_one, blocks[2]))
    self_context, self_log = attend_forward(
        self_queries, self_keys, self_values, own_seg, own_seg, query_rows, table
    )
    first = inputs + dot_plain(self_context, blocks[3])
    normed_two = to_half(rms_scale(first, gains[1]))
    cross_queries = to_half(dot_plain(normed_two, blocks[4]))
    cross_keys = to_half(dot_plain(encoded, blocks[5]))
    cross_values = to_half(dot_plain(encoded, blocks[6]))
    cross_context, cross_log = attend_forward(
        cross_queries, cross_keys, cross_values, enc_seg, own_seg, query_rows, None
    )
    second = first + dot_plain(cross_context, blocks[7])
    normed_three = to_half(rms_scale(second, gains[2]))
    gate_pre = dot_cols(normed_three, gate_rows)
    up_pre = dot_cols(normed_three, up_rows)
    gelu_value, gelu_pull = jax.vjp(gelu_tanh, gate_pre)
    hidden = to_half(gelu_value * up_pre)
    output = second + dot_plain(hidden, down_rows)
    scoring_again, weights_again, small_again, _ = lax.optimization_barrier(
        (scoring, weights, small_params, output)
    )
    full_scoring, full_weights, full_small = (
        lax.all_gather(scoring_again, ("dp", "fsdp"), axis=0, tiled=True),
        lax.all_gather(weights_again, ("dp", "fsdp"), axis=0, tiled=True),
        lax.all_gather(small_again, ("dp", "fsdp"), axis=0, tiled=True),
    )
    blocks, gate_rows, up_rows, down_rows, gains, table = unpack(
        full_scoring, full_weights, full_small
    )
    cot_half = to_half(cotangent)
    grad_down = dot_rows(hidden, cot_half)
    grad_hidden = dot_cols(cot_half, down_rows)
    grad_gate = to_half(gelu_pull(grad_hidden * up_pre)[0])
    grad_up = to_half(grad_hidden * gelu_value)
    grad_gate_rows = dot_rows(grad_gate, normed_three)
    grad_up_rows = dot_rows(grad_up, normed_three)
    grad_normed_three = dot_plain(grad_gate, gate_rows) + dot_plain(grad_up, up_rows)
    _, norm_pull = jax.vjp(rms_scale, second, gains[2])
    back_second, grad_gain_three = norm_pull(grad_normed_three)
    grad_second = cotangent + back_second
    second_half = to_half(grad_second)
    grad_cross_out = dot_rows(cross_context, second_half)
    grad_cross_context = to_half(dot_cols(second_half, blocks[7]))
    grad_cross_queries, grad_cross_keys, grad_cross_values, _ = attend_backward(
        cross_queries,
        cross_keys,
        cross_values,
        enc_seg,
        own_seg,
        query_rows,
        None,
        cross_log,
        cross_context,
        grad_cross_context,
    )
    cross_query_half = to_half(grad_cross_queries)
    cross_key_half = to_half(grad_cross_keys)
    cross_value_half = to_half(grad_cross_values)
    grad_cross_query = dot_rows(normed_two, cross_query_half)
    grad_cross_key = dot_rows(encoded, cross_key_half)
    grad_cross_value = dot_rows(encoded, cross_value_half)
    grad_encoded = dot_cols(cross_key_half, blocks[5]) + dot_cols(cross_value_half, blocks[6])
    grad_normed_two = dot_cols(cross_query_half, blocks[4])
    _, norm_pull_two = jax.vjp(rms_scale, first, gains[1])
    back_first, grad_gain_two = norm_pull_two(grad_normed_two)
    grad_first = grad_second + back_first
    first_half = to_half(grad_first)
    grad_self_out = dot_rows(self_context, first_half)
    grad_self_context = to_half(dot_cols(first_half, blocks[3]))
    grad_self_queries, grad_self_keys, grad_self_values, grad_table = attend_backward(
        self_queries,
        self_keys,
        self_values,
        own_seg,
        own_seg,
        query_rows,
        table,
        self_log,
        self_context,
        grad_self_context,
    )
    query_half = to_half(grad_self_queries)
    key_half = to_half(grad_self_keys)
    value_half = to_half(grad_self_values)
    grad_query = dot_rows(normed_one, query_half)
    grad_key = dot_rows(normed_one, key_half)
    grad_value = dot_rows(normed_one, value_half)
    grad_normed_one = (
        dot_cols(query_half, blocks[0])
        + dot_cols(key_half, blocks[1])
        + dot_cols(value_half, blocks[2])
    )
    _, norm_pull_one = jax.vjp(rms_scale, inputs, gains[0])
    back_input, grad_gain_one = norm_pull_one(grad_normed_one)
    grad_inputs = grad_first + back_input
    scoring_terms = jnp.concatenate(
        [grad_query, grad_key, grad_cross_query, grad_cross_key], axis=0
    )
    weight_terms = jnp.concatenate(
        [
            grad_value,
            grad_self_out,
            grad_cross_value,
            grad_cross_out,
            grad_gate_rows,
            grad_up_rows,
            grad_down,
        ],
        axis=0,
    )
    small_terms = jnp.concatenate(
        [grad_gain_one, grad_gain_two, grad_gain_three, grad_table.reshape(-1)]
    )
    grad_scoring, grad_weights, grad_small = (
        lax.psum_scatter(scoring_terms, ("dp", "fsdp"), scatter_dimension=0, tiled=True),
        lax.psum_scatter(weight_terms, ("dp", "fsdp"), scatter_dimension=0, tiled=True),
        lax.psum_scatter(small_terms, ("dp", "fsdp"), scatter_dimension=0, tiled=True),
    )
    return (output, grad_inputs, grad_encoded, grad_scoring, grad_weights, grad_small)


def solution(mesh):
    return jax.shard_map(
        per_device,
        mesh=mesh,
        in_specs=(
            P(("dp", "fsdp"), None),
            P(("dp", "fsdp"), None),
            P(("dp", "fsdp"), None),
            P(("dp", "fsdp"), None),
            P(("dp", "fsdp"), None),
            P(("dp", "fsdp")),
            P(("dp", "fsdp"), None),
            P(("dp", "fsdp"), None),
        ),
        out_specs=(
            P(("dp", "fsdp"), None),
            P(("dp", "fsdp"), None),
            P(("dp", "fsdp"), None),
            P(("dp", "fsdp"), None),
            P(("dp", "fsdp"), None),
            P(("dp", "fsdp")),
        ),
        check_vma=False,
    )
```

profile of v0, /device:TPU:0, one launch (start us, length us, event | category | flops | bytes accessed | tf_op | source)
XLA Modules:
  0.0 983.3 jit_solution(17087407765346639859)
XLA Ops:
  13.4 68.9 %all-reduce = bf16[2688]{0:T(1024)(128)(2,1)S(1)} all-reduce(bf16[2688]{0:T(1024)(128)(2,1)S(1)} %dynamic-update-slice), channel_id=1, replica_groups=mesh['dp'=16,'fsdp'=8] {'dp','fsdp'}, use_global_device_ids=true, to_apply=%add | all-reduce | flops 2688 | bytes 10752
  98.5 40.8 %while.80 = (s32[]{:T(128)}, f32[12,384]{1,0:T(8,128)S(1)}, f32[12,384]{1,0:T(8,128)S(1)}, s32[3,128]{1,0:T(4,128)}, s32[1,384]{1,0:T(1,128)S(1)}, /*index=5*/s3...) while((s32[]{:T(128)}, f32[12,384]{1,0:T(8,128)S(1)}, ...), condition=%wide.region_4.5_spmd.clone, body=%wide.region_1.4_spmd.clone.sunk | while | flops 119757440 | bytes 9000604 | solution.py:131
  102.2 9.6 fusion.385
  115.7 9.6 fusion.385
  129.2 9.6 fusion.385
  139.3 17.9 %all-gather.5.cloned.1.call-done = bf16[9216,768]{1,0:T(8,128)(2,1)} async-done(((bf16[72,768]{1,0:T(8,128)(2,1)}), bf16[9216,768]{1,0:T(8,128)(2,1)}) %all-gather.5.cloned.1.call-update) | async-done | bytes 14155792 | tf_op jit(solution)/shard_map/all_gather | solution.py:207
  167.1 52.9 %while.81 = (s32[]{:T(128)}, f32[384,12,64]{0,2,1:T(8,128)}, bf16[3,128,12,64]{1,3,2,0:T(8,128)(2,1)}, s32[3,128]{1,0:T(4,128)}, s32[1,384]{1,0:T(1,128)S(1)}, /...) while((s32[]{:T(128)}, f32[384,12,64]{0,2,1:T(8,128)}, ...), condition=%wide.region_6.7_spmd.clone, body=%wide.region_5.6_spmd.clone.sunk | while | flops 195821696 | bytes 6632342 | solution.py:145
  173.0 11.5 %fusion.392 = f32[384,12,64]{0,2,1:T(8,128)} fusion(bf16[384,12,64]{0,2,1:T(8,128)(2,1)S(1)} %get-tuple-element.1932, f32[384,12,64]{0,2,1:T(8,128)} %get-tuple-element.1914, f32[12,384]{1,0:T(8,128)S(1)} %get-tuple-element.1934, f32[12]{0:T(128)S(1)} %get-tuple-element.1694, f32[12]{0:T(128)} %get-tuple-element.1695, f32[12]{0:T(128)} %get-tuple-element.1696, ...), kind=kOutput, calls=%fused_computation.100.clone.1 | convolution fusion | flops 191692800 | bytes 4999776 | tf_op jit(solution)/shard_map/while/body/eval_jaxpr/hkq,khd->qhd/dot_general | solution.py:140
  190.0 12.1 %fusion.392 = f32[384,12,64]{0,2,1:T(8,128)} fusion(bf16[384,12,64]{0,2,1:T(8,128)(2,1)S(1)} %get-tuple-element.1932, f32[384,12,64]{0,2,1:T(8,128)} %get-tuple-element.1914, f32[12,384]{1,0:T(8,128)S(1)} %get-tuple-element.1934, f32[12]{0:T(128)S(1)} %get-tuple-element.1694, f32[12]{0:T(128)} %get-tuple-element.1695, f32[12]{0:T(128)} %get-tuple-element.1696, ...), kind=kOutput, calls=%fused_computation.100.clone.1 | convolution fusion | flops 191692800 | bytes 4999776 | tf_op jit(solution)/shard_map/while/body/eval_jaxpr/hkq,khd->qhd/dot_general | solution.py:140
  207.7 12.1 %fusion.392 = f32[384,12,64]{0,2,1:T(8,128)} fusion(bf16[384,12,64]{0,2,1:T(8,128)(2,1)S(1)} %get-tuple-element.1932, f32[384,12,64]{0,2,1:T(8,128)} %get-tuple-element.1914, f32[12,384]{1,0:T(8,128)S(1)} %get-tuple-element.1934, f32[12]{0:T(128)S(1)} %get-tuple-element.1694, f32[12]{0:T(128)} %get-tuple-element.1695, f32[12]{0:T(128)} %get-tuple-element.1696, ...), kind=kOutput, calls=%fused_computation.100.clone.1 | convolution fusion | flops 191692800 | bytes 4999776 | tf_op jit(solution)/shard_map/while/body/eval_jaxpr/hkq,khd->qhd/dot_general | solution.py:140
  226.9 5.0 while.82
  232.0 5.8 while.83
  244.4 6.2 multiply_convert_fusion
  251.8 4.3 fusion.234
  258.0 66.7 %all-reduce.1 = bf16[2688]{0:T(1024)(128)(2,1)S(1)} all-reduce(bf16[2688]{0:T(1024)(128)(2,1)S(1)} %dynamic-update-slice.1), channel_id=1, replica_groups=mesh['dp'=16,'fsdp'=8] {'dp','fsdp'}, use_global_device_ids=true, to_apply=%add.1 | all-reduce | flops 2688 | bytes 10752
  326.0 6.5 all-gather.9.cloned.1.call-done
  332.5 7.4 fusion.220
  348.7 20.4 %while.84 = (s32[]{:T(128)}, f32[384,12,64]{0,2,1:T(8,128)}, bf16[3,64,12,64]{3,1,2,0:T(8,128)(2,1)}, bf16[3,64,12,64]{3,1,2,0:T(8,128)(2,1)}, bf16[3,64,12,64]{...) while((s32[]{:T(128)}, f32[384,12,64]{0,2,1:T(8,128)}, ...), condition=%wide.region_18.19_spmd.clone, body=%wide.region_17.18_spmd.clone.sunk | while | flops 191422464 | bytes 25650780 | solution.py:192
  376.7 25.1 %all-gather.11.cloned.1.call-done = bf16[3072,768]{1,0:T(8,128)(2,1)} async-done(((bf16[24,768]{1,0:T(8,128)(2,1)}), bf16[3072,768]{1,0:T(8,128)(2,1)}) %all-gather.11.cloned.1.call-update) | async-done | bytes 4718608 | tf_op jit(solution)/shard_map/all_gather | solution.py:243
  412.4 79.2 %while.85 = (s32[]{:T(128)}, f32[384,12,64]{0,2,1:T(8,128)S(1)}, f32[32,12]{0,1:T(8,128)S(1)}, bf16[3,128,12,64]{1,3,2,0:T(8,128)(2,1)}, bf16[3,128,12,64]{1,3,2...) while((s32[]{:T(128)}, f32[384,12,64]{0,2,1:T(8,128)S(1)}, ...), condition=%wide.region_22.23_spmd.clone, body=%wide.region_21.22_spmd.clone.sunk | while | flops 655147904 | bytes 35825596 | solution.py:192
  420.8 9.8 exponential_select_fusion.2
  433.1 4.2 fusion.431
  447.1 9.8 exponential_select_fusion.2
  459.4 4.2 fusion.431
  473.4 9.8 exponential_select_fusion.2
  485.6 4.2 fusion.431
  513.1 4.5 convolution_dynamic-update-slice_fusion.2
  517.6 4.5 convolution_dynamic-update-slice_fusion.1
  522.1 4.5 convolution_dynamic-update-slice_fusion
  535.3 62.9 %all-reduce.2 = f32[2688]{0:T(1024)S(1)} all-reduce(f32[2688]{0:T(1024)S(1)} %pad_maximum_fusion.1), channel_id=4, replica_groups=mesh['dp'=16,'fsdp'=8] {'dp','fsdp'}, use_global_device_ids=true, to_apply=%region_29.30.clone | all-reduce | flops 2688 | bytes 21504
  604.7 110.4 %reduce-scatter.3.cloned.1.call-done = f32[24,768]{1,0:T(8,128)} async-done(((f32[3072,768]{1,0:T(8,128)}), f32[24,768]{1,0:T(8,128)}) %reduce-scatter.3.cloned.1.call-update) | async-done | bytes 73744 | tf_op jit(solution)/shard_map/reduce_scatter | solution.py:335
  715.2 261.0 %reduce-scatter.5.cloned.1.call-done = f32[72,768]{1,0:T(8,128)} async-done(((f32[9216,768]{1,0:T(8,128)}), f32[72,768]{1,0:T(8,128)}) %reduce-scatter.5.cloned.1.call-update) | async-done | bytes 221200 | tf_op jit(solution)/shard_map/reduce_scatter | solution.py:336
  (478 shorter events, 208.3 us)
Async XLA Ops:
  7.2 79.4 %copy-start = (bf16[192,768]{1,0:T(8,128)(2,1)S(1)}, bf16[192,768]{1,0:T(8,128)(2,1)}, u32[]{:S(2)}) copy-start(bf16[192,768]{1,0:T(8,128)(2,1)} %param.21) | copy-start | bytes 884740
  7.2 79.3 %all-gather.7.cloned.1.call-start = ((), (), s32[]{:S(2)}) async-start(), calls=%async_computation.3 | async-start | bytes 4755456 | tf_op jit(solution)/shard_map/all_gather | solution.py:206
  7.9 149.3 %all-gather.5.cloned.1.call-start = ((), (), s32[]{:S(2)}) async-start(), calls=%async_computation.2 | async-start | bytes 14266368 | tf_op jit(solution)/shard_map/all_gather | solution.py:207
  8.7 323.8 %all-gather.9.cloned.1.call-start = ((), (), s32[]{:S(2)}) async-start(), calls=%async_computation.4 | async-start | bytes 14266368 | tf_op jit(solution)/shard_map/all_gather | solution.py:244
  86.5 74.2 %copy-start.17 = (bf16[384,768]{1,0:T(8,128)(2,1)}, bf16[384,768]{1,0:T(8,128)(2,1)S(1)}, u32[]{:S(2)}) copy-start(bf16[384,768]{1,0:T(8,128)(2,1)S(1)} %multiply_convert_fusion.3) | copy-start | bytes 1769476
  167.1 54.3 %copy-start.5 = (f32[384,768]{1,0:T(8,128)S(1)}, f32[384,768]{1,0:T(8,128)}, u32[]{:S(2)}) copy-start(f32[384,768]{1,0:T(8,128)} %param.20) | copy-start | bytes 3538948
  173.0 11.6 %copy-start.74 = (s32[3]{0:T(128)S(1)}, s32[3]{0:T(128)}, u32[]{:S(2)}) copy-start(s32[3]{0:T(128)} %copy-done.73) | copy-start | bytes 40 | tf_op jit(solution)/shard_map/while
  190.0 12.1 %copy-start.74 = (s32[3]{0:T(128)S(1)}, s32[3]{0:T(128)}, u32[]{:S(2)}) copy-start(s32[3]{0:T(128)} %copy-done.73) | copy-start | bytes 40 | tf_op jit(solution)/shard_map/while
  207.6 12.1 %copy-start.74 = (s32[3]{0:T(128)S(1)}, s32[3]{0:T(128)}, u32[]{:S(2)}) copy-start(s32[3]{0:T(128)} %copy-done.73) | copy-start | bytes 40 | tf_op jit(solution)/shard_map/while
  221.3 5.2 copy-start.21
  226.9 5.1 copy-start.1
  240.4 10.2 %copy-start.14 = (f32[384,768]{1,0:T(8,128)}, f32[384,768]{1,0:T(8,128)S(1)}, u32[]{:S(2)}) copy-start(f32[384,768]{1,0:T(8,128)S(1)} %get-tuple-element.1092) | copy-start | bytes 3538948
  244.4 6.2 copy-start.78
  251.8 6.0 copy-start.72
  256.1 145.7 %all-gather.11.cloned.1.call-start = ((), (), s32[]{:S(2)}) async-start(), calls=%async_computation.5 | async-start | bytes 4755456 | tf_op jit(solution)/shard_map/all_gather | solution.py:243
  256.7 458.5 %reduce-scatter.3.cloned.1.call-start = ((), (), s32[]{:S(2)}) async-start(), calls=%async_computation.6 | async-start | bytes 9510912 | tf_op jit(solution)/shard_map/reduce_scatter | solution.py:335
  332.5 8.1 copy-start.43
  376.7 28.0 %copy-start.10 = (f32[384,768]{1,0:T(8,128)S(1)}, f32[384,768]{1,0:T(8,128)}, u32[]{:S(2)}) copy-start(f32[384,768]{1,0:T(8,128)} %copy-done.9) | copy-start | bytes 3538948
  406.1 6.3 copy-start.4
  406.1 6.3 copy-start.33
  406.1 6.3 copy-start.76
  420.8 9.8 copy-start.47
  447.1 9.8 copy-start.47
  473.4 9.8 copy-start.47
  500.8 475.3 %reduce-scatter.5.cloned.1.call-start = ((), (), s32[]{:S(2)}) async-start(), calls=%async_computation.7 | async-start | bytes 28532736 | tf_op jit(solution)/shard_map/reduce_scatter | solution.py:336
  502.7 6.2 copy-start.37
  513.1 4.5 copy-start.40
  517.6 4.5 copy-start.31
  517.6 4.5 copy-start.35
  532.1 66.7 %copy-start.64 = (f32[384]{0:T(512)S(1)}, f32[384]{0:T(512)}, u32[]{:S(2)}) copy-start(f32[384]{0:T(512)} %copy-done.63) | copy-start | bytes 4612
  532.1 68.7 %copy-start.38 = (bf16[192,768]{1,0:T(8,128)(2,1)S(1)}, bf16[192,768]{1,0:T(8,128)(2,1)}, u32[]{:S(2)}) copy-start(bf16[192,768]{1,0:T(8,128)(2,1)} %copy-done.37) | copy-start | bytes 884740
  598.8 4.6 copy-start.32
  (81 other events, 173.8 us)
Sparse Core Ops, SparseCore 0:
  11.1 69.7 all-gather.6
  84.0 73.1 all-gather.4
  256.2 76.2 all-gather.8
  335.4 66.3 all-gather.10
  500.9 214.1 reduce-scatter.2
  721.0 255.0 reduce-scatter.4
where the time goes:
time: 991 us; the launch traced here: 983 us
  waiting for transfers between devices  423 us (43%)
  matrix products  232 us (23%)
  blocking collectives  198 us (20%)
  local copies, waits for them, and re-layouts  62.4 us (6%)
  other arithmetic  49.3 us (5%)
  between operations  15.5 us (2%)
    reduce_scatter x1, waiting for transfers between devices, per_device(): lax.psum_scatter(weight_terms, ('dp', 'fsdp'), scatter_dimension=0, tiled...  261 us
    unnamed x3, blocking collectives  198 us
    reduce_scatter x1, waiting for transfers between devices, per_device(): lax.psum_scatter(scoring_terms, ('dp', 'fsdp'), scatter_dimension=0, tile...  110 us
    dot_general x12, matrix products, block_scores(): jnp.einsum('khd,qhd->hkq', key_block, query_heads, preferred_element_type...  66.1 us
    dot_general x6, matrix products, second_pass(): jnp.einsum('hkq,khd->qhd', to_half(probs), value_block, preferred_element...  41 us
    dot_general x11, matrix products, dot_cols(): lax.dot_general(left, right, (((1,), (1,)), ((), ())), preferred_element_...  36.7 us
    dot_general x11, matrix products, dot_rows(): lax.dot_general(left, right, (((0,), (0,)), ((), ())), preferred_element_...  27.6 us
    dot_general x11, matrix products, dot_plain(): return jnp.dot(left, right, preferred_element_type=jnp.float32)  25.4 us
  transfers between devices with their start and end apart: 6, of which 5 were waited for; matrix products, arithmetic and copies ran while one was open for 14% of the time, Pallas kernels for 0%

commit v1 on v0

v1 whole, which is shorter than its diff:
```python
import jax
import jax.numpy as jnp
import numpy as np
from jax import lax
from jax.experimental import pallas as pl
from jax.experimental.pallas import tpu as pltpu
from jax.sharding import PartitionSpec as P

MESH_ID = pl.DeviceIdType.MESH
D = 768
SC_ROWS = 24
WT_ROWS = 72
RING_ORDERS = ((0, 1, 2), (1, 2, 0), (2, 0, 1))
PART_FULL = (((0, 0, 24), (1, 0, 8)), ((1, 8, 32), (2, 0, 8)), ((1, 40, 32),))
PART_LOW = (((0, 0, 16),), ((1, 8, 16), (2, 0, 8)), ((1, 40, 16),))
PART_HIGH = (((0, 16, 8), (1, 0, 8)), ((1, 24, 16),), ((1, 56, 16),))


def grid_place():
    dp = lax.axis_index("dp")
    fs = lax.axis_index("fsdp")
    return [dp // 4, dp % 4, fs // 2], fs % 2


def device_at(place, core):
    return (place[0] * 4 + place[1], place[2] * 2 + core)


def shifted(place, axis, step):
    moved = list(place)
    moved[axis] = (place[axis] + step + 4) % 4
    return moved


def ring_barrier(place, core):
    barrier = pltpu.get_barrier_semaphore()
    for axis in range(3):
        for step in (1, -1):
            pl.semaphore_signal(
                barrier, inc=1, device_id=device_at(shifted(place, axis, step), core), device_id_type=MESH_ID
            )
    pl.semaphore_signal(barrier, inc=1, device_id=device_at(place, 1 - core), device_id_type=MESH_ID)
    pl.semaphore_wait(barrier, 7)


def gather_kernel(sc_in, wt_in, sm_in, sc_out, wt_out, sm_out, local_sem, send_sem, recv_sem):
    place, core = grid_place()
    ins = (sc_in, wt_in, sm_in)
    outs = (sc_out, wt_out, sm_out)
    local = [
        pltpu.make_async_copy(ins[i], outs[i].at[place[0], place[1], place[2], core], local_sem.at[i])
        for i in range(3)
    ]
    for copy in local:
        copy.start()
    ring_barrier(place, core)
    used = [0]
    sends = []

    def block(piece, index):
        array, first, rows = piece
        return outs[array].at[tuple(index) + (core, pl.ds(first, rows))]

    def push(pieces, index, target, from_input=False):
        got = []
        for piece in pieces:
            slot = used[0]
            used[0] += 1
            dst = block(piece, index)
            src = ins[piece[0]].at[pl.ds(piece[1], piece[2])] if from_input else dst
            copy = pltpu.make_async_remote_copy(
                src_ref=src,
                dst_ref=dst,
                send_sem=send_sem.at[slot],
                recv_sem=recv_sem.at[slot],
                device_id=target,
                device_id_type=MESH_ID,
            )
            copy.start()
            sends.append(copy)
            got.append(copy)
        return got

    def arrive(copies):
        for copy in copies:
            copy.wait_recv()

    sibling = device_at(place, 1 - core)
    cross = []
    for stage in range(3):
        first = []
        for part in range(3):
            order = RING_ORDERS[part]
            axis = order[stage]
            index = [slice(None) if order.index(k) < stage else place[k] for k in range(3)]
            up = push(PART_FULL[part], index, device_at(shifted(place, axis, 1), core), stage == 0)
            down = push(PART_FULL[part], index, device_at(shifted(place, axis, -1), core), stage == 0)
            first.append((axis, index, up, down))
        if stage == 0:
            for part in range(3):
                cross += push(PART_FULL[part], place, sibling, True)
            for copy in local:
                copy.wait()
        second = []
        for part in range(3):
            axis, index, up, down = first[part]
            left = list(index)
            left[axis] = (place[axis] + 3) % 4
            right = list(index)
            right[axis] = (place[axis] + 1) % 4
            arrive(up)
            up2 = push(PART_LOW[part], left, device_at(shifted(place, axis, 1), core))
            cross += push(PART_FULL[part], left, sibling)
            arrive(down)
            down2 = push(PART_HIGH[part], right, device_at(shifted(place, axis, -1), core))
            cross += push(PART_FULL[part], right, sibling)
            second.append((axis, index, up2, down2))
        for part in range(3):
            axis, index, up2, down2 = second[part]
            far = list(index)
            far[axis] = (place[axis] + 2) % 4
            arrive(up2)
            cross += push(PART_LOW[part], far, sibling)
            arrive(down2)
            cross += push(PART_HIGH[part], far, sibling)
    arrive(cross)
    for copy in sends:
        copy.wait_send()


GATHER_COPIES = 5 + 3 * 36


def gather_params(scoring, weights, small):
    small_tile = jnp.pad(small.reshape(1, 21), ((0, 7), (0, 107)))
    any_spec = pl.BlockSpec(memory_space=pl.ANY)
    full_sc, full_wt, full_sm = pl.pallas_call(
        gather_kernel,
        out_shape=(
            jax.ShapeDtypeStruct((4, 4, 4, 2, SC_ROWS, D), jnp.bfloat16),
            jax.ShapeDtypeStruct((4, 4, 4, 2, WT_ROWS, D), jnp.bfloat16),
            jax.ShapeDtypeStruct((4, 4, 4, 2, 8, 128), jnp.bfloat16),
        ),
        in_specs=[any_spec] * 3,
        out_specs=(any_spec,) * 3,
        scratch_shapes=[
            pltpu.SemaphoreType.DMA((3,)),
            pltpu.SemaphoreType.DMA((GATHER_COPIES,)),
            pltpu.SemaphoreType.DMA((GATHER_COPIES,)),
        ],
        compiler_params=pltpu.CompilerParams(collective_id=0, has_side_effects=True),
        name="gather_params",
    )(scoring, weights, small_tile)
    return (
        full_sc.reshape(3072, D),
        full_wt.reshape(9216, D),
        full_sm[..., 0, :21].reshape(2688),
    )


RS_FULL = (((0, 0, 24), (1, 0, 8)), ((1, 8, 32),), ((1, 40, 32),))
RS_LOW = (((0, 0, 16),), ((1, 8, 16),), ((1, 40, 16),))
RS_HIGH = (((0, 16, 8), (1, 0, 8)), ((1, 24, 16),), ((1, 56, 16),))


def scatter_kernel(g_sc, g_wt, g_sm, o_sc, o_wt, o_sm, acc_sc, acc_wt, sib_sc, sib_wt, bufs, small_own, small_in,
                   local_sem, send_sem, recv_sem):
    place, core = grid_place()
    grads = (g_sc, g_wt)
    accs = (acc_sc, acc_wt)
    sibs = (sib_sc, sib_wt)
    used = [0]
    sends = []

    def push(src, dst, target):
        slot = used[0]
        used[0] += 1
        copy = pltpu.make_async_remote_copy(
            src_ref=src, dst_ref=dst, send_sem=send_sem.at[slot], recv_sem=recv_sem.at[slot],
            device_id=target, device_id_type=MESH_ID,
        )
        copy.start()
        sends.append(copy)
        return copy

    sibling = device_at(place, 1 - core)
    pieces0 = [piece for part in RS_FULL for piece in part]
    own = []
    for i, (array, first, rows) in enumerate(pieces0):
        copy = pltpu.make_async_copy(
            grads[array].at[:, :, :, core, pl.ds(first, rows)],
            accs[array].at[:, :, :, pl.ds(first, rows)],
            local_sem.at[i],
        )
        copy.start()
        own.append(copy)
    small_copy = pltpu.make_async_copy(g_sm, small_own, local_sem.at[len(pieces0)])
    small_copy.start()
    ring_barrier(place, core)
    from_sib = []
    for array, first, rows in pieces0:
        from_sib.append(
            push(
                grads[array].at[:, :, :, 1 - core, pl.ds(first, rows)],
                sibs[array].at[:, :, :, pl.ds(first, rows)],
                sibling,
            )
        )
    small_copy.wait()
    small_first = push(small_own, small_in.at[0], sibling)

    def add_all(array, first, rows):
        def body(n, carry):
            a, b, e = n // 16, (n // 4) % 4, n % 4
            here = (a, b, e, pl.ds(first, rows))
            total = accs[array][here].astype(jnp.float32) + sibs[array][here].astype(jnp.float32)
            accs[array][here] = total.astype(jnp.bfloat16)
            return carry

        lax.fori_loop(0, 64, body, 0)

    def acc_at(piece, index):
        array, first, rows = piece
        return accs[array].at[tuple(index) + (pl.ds(first, rows),)]

    def add_into(piece, index, buf, free_axes, final=None):
        array, first, rows = piece
        count = 4 ** len(free_axes)

        def body(n, carry):
            here = list(index)
            local = []
            for position, axis in enumerate(free_axes):
                coord = (n // (4 ** (len(free_axes) - 1 - position))) % 4
                here[axis] = coord
                local.append(coord)
            where = tuple(here) + (pl.ds(first, rows),)
            total = accs[array][where].astype(jnp.float32) + buf[tuple(local) + (slice(None),)].astype(jnp.float32)
            accs[array][where] = total.astype(jnp.bfloat16)
            return carry

        lax.fori_loop(0, count, body, 0)

    buf_at = [0]

    def take_buf():
        buf = bufs[buf_at[0]]
        buf_at[0] += 1
        return buf

    count = 0
    state = {}
    for stage in range(3):
        for part in range(3):
            order = RING_ORDERS[part]
            axis = order[stage]
            free = sorted(order[stage + 1:])
            index = [slice(None) if k in free else place[k] for k in range(3)]
            if stage == 0:
                for piece in RS_FULL[part]:
                    own[count].wait()
                    from_sib[count].wait_recv()
                    add_all(*piece)
                    count += 1
            far = list(index)
            far[axis] = (place[axis] + 2) % 4
            up_dev = device_at(shifted(place, axis, 1), core)
            down_dev = device_at(shifted(place, axis, -1), core)
            low = []
            for piece in RS_LOW[part]:
                buf = take_buf()
                low.append((piece, buf, push(acc_at(piece, far), buf, up_dev)))
            high = []
            for piece in RS_HIGH[part]:
                buf = take_buf()
                high.append((piece, buf, push(acc_at(piece, far), buf, down_dev)))
            state[part] = (axis, free, index, up_dev, down_dev, low, high)
        if stage == 0:
            small_first.wait_recv()
            small_own2 = small_own[...] + small_in[0]
        for part in range(3):
            axis, free, index, up_dev, down_dev, low, high = state[part]
            right = list(index)
            right[axis] = (place[axis] + 1) % 4
            left = list(index)
            left[axis] = (place[axis] + 3) % 4
            for piece, buf, copy in low:
                copy.wait_recv()
                add_into(piece, right, buf, free)
            ups = []
            for piece in RS_FULL[part]:
                buf = take_buf()
                ups.append((piece, buf, push(acc_at(piece, right), buf, up_dev)))
            for piece, buf, copy in high:
                copy.wait_recv()
                add_into(piece, left, buf, free)
            downs = []
            for piece in RS_FULL[part]:
                buf = take_buf()
                downs.append((piece, buf, push(acc_at(piece, left), buf, down_dev)))
            state[part] = (axis, free, index, ups, downs)
        for part in range(3):
            axis, free, index, ups, downs = state[part]
            if stage < 2:
                for piece, buf, copy in ups + downs:
                    copy.wait_recv()
                    add_into(piece, index, buf, free)
            else:
                for (piece, buf, copy), (_, buf2, copy2) in zip(ups, downs):
                    copy.wait_recv()
                    copy2.wait_recv()
                    array, first, rows = piece
                    out = (o_sc, o_wt)[array]
                    out[pl.ds(first, rows)] = (
                        accs[array][tuple(place) + (pl.ds(first, rows),)].astype(jnp.float32)
                        + buf[...].astype(jnp.float32)
                        + buf2[...].astype(jnp.float32)
                    )
    for axis in range(3):
        small_copy_ref = small_in.at[1 + 4 * axis]
        small_copy_ref[...] = small_own2
        got = []
        for k, step in enumerate((1, -1, 2)):
            got.append(
                push(small_copy_ref, small_in.at[2 + 4 * axis + k], device_at(shifted(place, axis, step), core))
            )
        for copy in got:
            copy.wait_recv()
        small_own2 = small_own2 + small_in[2 + 4 * axis] + small_in[3 + 4 * axis] + small_in[4 + 4 * axis]
    o_sm[...] = small_own2
    for copy in sends:
        copy.wait_send()


def rs_buffers():
    shapes = []
    for stage in range(3):
        lead = (4,) * (2 - stage)
        for part in range(3):
            for piece in RS_LOW[part] + RS_HIGH[part]:
                shapes.append(pltpu.VMEM(lead + (piece[2], D), jnp.bfloat16))
        for part in range(3):
            for piece in RS_FULL[part] * 2:
                shapes.append(pltpu.VMEM(lead + (piece[2], D), jnp.bfloat16))
    return shapes


SCATTER_COPIES = 4 + 1 + 3 * (7 + 8) + 9


def scatter_grads(g_sc, g_wt, g_small):
    any_spec = pl.BlockSpec(memory_space=pl.ANY)
    vmem = pl.BlockSpec(memory_space=pltpu.VMEM)
    small = jnp.pad(g_small.reshape(21, 128), ((0, 3), (0, 0)))
    o_sc, o_wt, o_sm = pl.pallas_call(
        scatter_kernel,
        out_shape=(
            jax.ShapeDtypeStruct((SC_ROWS, D), jnp.float32),
            jax.ShapeDtypeStruct((WT_ROWS, D), jnp.float32),
            jax.ShapeDtypeStruct((24, 128), jnp.float32),
        ),
        in_specs=[any_spec] * 3,
        out_specs=(vmem,) * 3,
        scratch_shapes=[
            pltpu.VMEM((4, 4, 4, SC_ROWS, D), jnp.bfloat16),
            pltpu.VMEM((4, 4, 4, WT_ROWS, D), jnp.bfloat16),
            pltpu.VMEM((4, 4, 4, SC_ROWS, D), jnp.bfloat16),
            pltpu.VMEM((4, 4, 4, WT_ROWS, D), jnp.bfloat16),
            rs_buffers(),
            pltpu.VMEM((24, 128), jnp.float32),
            pltpu.VMEM((13, 24, 128), jnp.float32),
            pltpu.SemaphoreType.DMA((5,)),
            pltpu.SemaphoreType.DMA((SCATTER_COPIES,)),
            pltpu.SemaphoreType.DMA((SCATTER_COPIES,)),
        ],
        compiler_params=pltpu.CompilerParams(
            collective_id=1, has_side_effects=True, vmem_limit_bytes=56 << 20
        ),
        name="scatter_grads",
    )(g_sc.reshape(4, 4, 4, 2, SC_ROWS, D), g_wt.reshape(4, 4, 4, 2, WT_ROWS, D), small)
    me = lax.axis_index("dp") * 8 + lax.axis_index("fsdp")
    mine = lax.dynamic_slice(o_sm.reshape(-1), (me * 21,), (21,))
    return o_sc, o_wt, mine
FF = 2048
H = 12
BUCKETS = 32
ROWS = 384
KEYS = 192
PAIRS = 6
CH = 256
SPAN = 640
EPSILON = 1e-06
MASKED_SCORE = -1e30
BUCKET_EDGES = [int(e) for e in np.ceil(16.0 * 8.0 ** ((np.arange(17, 32) - 16) / 16.0))]
SELF_AT = (0, 128, 384)
LOG2 = float(np.sqrt(2.0 / np.pi))
BLOCKS = ("wq", "wk", "wv", "wo", "ck", "cv", "cq", "co", "gt", "ut", "dn")
PLACE = {
    "wq": (0, 0, 768), "wk": (0, 768, 768), "cq": (0, 1536, 768), "ck": (0, 2304, 768),
    "wv": (1, 0, 768), "wo": (1, 768, 768), "cv": (1, 1536, 768), "co": (1, 2304, 768),
    "gt": (1, 3072, FF), "ut": (1, 5120, FF), "dn": (1, 7168, FF),
}


def f32(v):
    return v.astype(jnp.float32)


def half(v):
    return v.astype(jnp.bfloat16)


def dot_nn(a, b):
    return lax.dot_general(a, b, (((1,), (0,)), ((), ())), preferred_element_type=jnp.float32)


def dot_nt(a, b):
    return lax.dot_general(a, b, (((1,), (1,)), ((), ())), preferred_element_type=jnp.float32)


def dot_tn(a, b):
    return lax.dot_general(a, b, (((0,), (0,)), ((), ())), preferred_element_type=jnp.float32)


def lane_roll_rows(base, sign):
    rows = lax.broadcasted_iota(jnp.int32, base.shape, 0)
    for bit in range(3):
        step = (1 << bit) if sign > 0 else 256 - (1 << bit)
        base = jnp.where((rows >> bit) % 2 == 1, pltpu.roll(base, step, 1), base)
    return base


def layer_kernel(
    x, enc, cot, gains, table, seg, eseg, w_sc, w_wt,
    out, g_in, g_enc, g_sc, g_wt, g_gain, g_table,
    sc, wt, bias, smask, cmask, p1, p2, n1, q1, k1, v1, c1, y1, n2, q2, k2, v2, c2, y2, n3, cb,
    t1, t2, t3, dqs, dks, dvs, dk2s, dv2s, dn_acc, acc_k, acc_v, diag, hid, das, dbs, stage,
    w_sem, s_sem,
):
    vm = (sc, wt)
    hb = (w_sc, w_wt)
    copies = {}
    for i, name in enumerate(BLOCKS):
        array, first, rows = PLACE[name]
        copies[name] = pltpu.make_async_copy(
            hb[array].at[pl.ds(first, rows)], vm[array].at[pl.ds(first, rows)], w_sem.at[i]
        )
        copies[name].start()

    def weight(name):
        array, first, rows = PLACE[name]
        return vm[array].at[pl.ds(first, rows)]

    def need(*names):
        for name in names:
            copies[name].wait()

    def rows_loop(total, body, step=128):
        def run(i, carry):
            body(pl.ds(pl.multiple_of(i * step, step), step))
            return carry

        lax.fori_loop(0, total // step, run, 0)

    def cols_loop(total, body, step=CH):
        def run(i, carry):
            body(pl.ds(pl.multiple_of(i * step, step), step))
            return carry

        lax.fori_loop(0, total // step, run, 0)

    def rms_into(dst, src, row):
        def body(at):
            v = src[at, :]
            inv = lax.rsqrt(jnp.mean(v * v, axis=-1, keepdims=True) + EPSILON)
            dst[at, :] = half(v * inv * gains[row : row + 1, :])

        rows_loop(ROWS, body)

    def rms_back(dst, base, src, dn, row):
        g_gain[row : row + 1, :] = jnp.zeros((1, D), jnp.float32)

        def body(at):
            v = src[at, :]
            d = dn[at, :]
            inv = lax.rsqrt(jnp.mean(v * v, axis=-1, keepdims=True) + EPSILON)
            normed = v * inv
            g_gain[row : row + 1, :] += jnp.sum(d * normed, axis=0, keepdims=True)
            dg = d * gains[row : row + 1, :]
            dst[at, :] = base[at, :] + inv * (dg - normed * jnp.mean(dg * normed, axis=-1, keepdims=True))

        rows_loop(ROWS, body)

    def project(dst, src, name):
        w = weight(name)

        def body(at):
            dst[:, at] = half(dot_nn(src[...], w[:, at]))

        cols_loop(D, body)

    chunk_no = [0]

    def leave(value, array, first, slot, fresh):
        if not fresh:
            pltpu.make_async_copy(stage.at[slot], (g_sc, g_wt)[array].at[pl.ds(0, CH)], s_sem.at[slot]).wait()
        stage[slot] = half(value)
        pltpu.make_async_copy(
            stage.at[slot], (g_sc, g_wt)[array].at[pl.ds(pl.multiple_of(first, CH), CH)], s_sem.at[slot]
        ).start()

    def weight_grad(lhs, rhs, name):
        array, first, rows = PLACE[name]
        steps = rows // CH

        for i in range(steps):
            slot = chunk_no[0] % 3
            leave(dot_tn(lhs[:, i * CH : (i + 1) * CH], rhs[...]), array, first + i * CH, slot, chunk_no[0] < 3)
            chunk_no[0] += 1

    need("wq", "wk", "wv")
    distance = lax.broadcasted_iota(jnp.int32, (BUCKETS, SPAN), 1) - 128
    unit = lax.broadcasted_iota(jnp.int32, (BUCKETS, SPAN), 0)
    far = jnp.zeros_like(distance)
    for edge in BUCKET_EDGES:
        far = far + (distance >= edge).astype(jnp.int32)
    bucket = jnp.where(distance < 16, distance, 16 + far)
    one_hot = half((bucket == unit).astype(jnp.float32))
    row_bias = dot_nn(table[...], one_hot)
    row_bias = jnp.where(lax.broadcasted_iota(jnp.int32, (16, SPAN), 1) < 128, MASKED_SCORE, row_bias)
    diag[...] = row_bias

    def make_bias(h, carry):
        row = diag[pl.ds(h, 1), :]
        for delta in range(3):
            base = lane_roll_rows(
                jnp.broadcast_to(row[:, delta * 128 : delta * 128 + 256], (8, 256)), 1
            )
            for a in range(16):
                rolled = base if a == 0 else pltpu.roll(base, 8 * a, 1)
                bias[h, delta, a * 8 : a * 8 + 8, :] = rolled[:, 128:]
        return carry

    lax.fori_loop(0, H, make_bias, 0)
    seg_f = jnp.broadcast_to(f32(seg[...]), (ROWS, ROWS))
    smask[...] = jnp.where(seg_f.T == seg_f, 0.0, MASKED_SCORE)
    enc_f = jnp.broadcast_to(f32(eseg[...]), (128, KEYS)).T
    cmask[...] = jnp.where(
        jnp.concatenate([enc_f, enc_f, enc_f], axis=1) == jnp.broadcast_to(f32(seg[...]), (KEYS, ROWS)),
        0.0, MASKED_SCORE,
    )
    lanes_of = lax.broadcasted_iota(jnp.int32, (1, 128), 1) // 64

    def pick(v, e):
        return jnp.where(lanes_of == e, v, jnp.zeros_like(v))

    rms_into(n1, x, 0)
    project(q1, n1, "wq")
    project(k1, n1, "wk")
    project(v1, n1, "wv")

    def self_forward(pair, carry):
        lanes = pl.ds(pl.multiple_of(pair * 128, 128), 128)
        q = q1[:, lanes]
        k = k1[:, lanes]
        vt = v1[:, lanes].T
        tops = [[None, None] for _ in range(3)]
        for e in range(2):
            h = pair * 2 + e
            km = pick(k, e)
            for i in range(3):
                n = (i + 1) * 128
                s = dot_nt(km[:n], q[i * 128 : (i + 1) * 128])
                s = s + jnp.concatenate([bias[h, i - j] for j in range(i + 1)], axis=0)
                s = s + smask[:n, i * 128 : (i + 1) * 128]
                top = jnp.max(s, axis=0, keepdims=True)
                ex = jnp.exp(s - top)
                p = ex * (1.0 / jnp.sum(ex, axis=0, keepdims=True))
                p1[h, SELF_AT[i] : SELF_AT[i] + n, :] = p
                tops[i][e] = dot_nn(vt[e * 64 : (e + 1) * 64, :n], half(p))
        for i in range(3):
            c1[i * 128 : (i + 1) * 128, lanes] = half(jnp.concatenate(tops[i], axis=0).T)
        return carry

    lax.fori_loop(0, PAIRS, self_forward, 0)
    need("wo")

    def first_body(at):
        y1[:, at] = x[:, at] + dot_nn(c1[...], weight("wo")[:, at])

    cols_loop(D, first_body)

    rms_into(n2, y1, 1)
    need("cq", "ck", "cv")
    project(q2, n2, "cq")
    project(k2, enc, "ck")
    project(v2, enc, "cv")

    def cross_forward(pair, carry):
        lanes = pl.ds(pl.multiple_of(pair * 128, 128), 128)
        q = q2[:, lanes]
        k = k2[:, lanes]
        vt = v2[:, lanes].T
        tops = []
        for e in range(2):
            h = pair * 2 + e
            s = dot_nt(pick(k, e), q) + cmask[...]
            top = jnp.max(s, axis=0, keepdims=True)
            ex = jnp.exp(s - top)
            p = ex * (1.0 / jnp.sum(ex, axis=0, keepdims=True))
            p2[h] = p
            tops.append(dot_nn(vt[e * 64 : (e + 1) * 64, :], half(p)))
        c2[:, lanes] = half(jnp.concatenate(tops, axis=0).T)
        return carry

    lax.fori_loop(0, PAIRS, cross_forward, 0)
    need("co")

    def second_body(at):
        y2[:, at] = y1[:, at] + dot_nn(c2[...], weight("co")[:, at])

    cols_loop(D, second_body)

    rms_into(n3, y2, 2)

    def start_body(at):
        cb[at, :] = half(cot[at, :])
        out[at, :] = y2[at, :]
        dn_acc[at, :] = jnp.zeros((128, D), jnp.float32)

    rows_loop(ROWS, start_body)
    need("gt", "ut", "dn")
    gt, ut, dn = weight("gt"), weight("ut"), weight("dn")

    def ffn(i, carry):
        at = pl.ds(pl.multiple_of(i * CH, CH), CH)
        g_rows = gt[at, :]
        u_rows = ut[at, :]
        d_rows = dn[at, :]
        a = dot_nt(n3[...], g_rows)
        b = dot_nt(n3[...], u_rows)
        dh = dot_nt(cb[...], d_rows)
        inner = jnp.tanh(LOG2 * (a + 0.044715 * a * a * a))
        gelu = 0.5 * a * (1.0 + inner)
        slope = 0.5 * (1.0 + inner) + 0.5 * a * (1.0 - inner * inner) * (LOG2 * (1.0 + 3 * 0.044715 * a * a))
        hid[...] = half(gelu * b)
        das[...] = half(dh * b * slope)
        dbs[...] = half(dh * gelu)
        out[...] += dot_nn(hid[...], d_rows)
        dn_acc[...] += dot_nn(das[...], g_rows) + dot_nn(dbs[...], u_rows)
        for slot, (lhs, rhs, name) in enumerate(((hid, cb, "dn"), (das, n3, "gt"), (dbs, n3, "ut"))):
            array, first, _ = PLACE[name]

            @pl.when(i > 0)
            def _():
                pltpu.make_async_copy(stage.at[slot], g_wt.at[pl.ds(0, CH)], s_sem.at[slot]).wait()

            stage[slot] = half(dot_tn(lhs[...], rhs[...]))
            pltpu.make_async_copy(
                stage.at[slot], g_wt.at[pl.ds(pl.multiple_of(first + i * CH, CH), CH)], s_sem.at[slot]
            ).start()
        return carry

    lax.fori_loop(0, FF // CH, ffn, 0)
    chunk_no[0] = 24
    rms_back(t1, cot, y2, dn_acc, 2)

    def to_half_rows(dst, src):
        def body(at):
            dst[at, :] = half(src[at, :])

        rows_loop(ROWS, body)

    to_half_rows(cb, t1)
    weight_grad(c2, cb, "co")

    def back_project(dst, src, name):
        w = weight(name)

        def body(at):
            dst[:, at] = half(dot_nt(src[...], w[at, :]))

        cols_loop(D, body)

    back_project(t3, cb, "co")

    def cross_backward(pair, carry):
        lanes = pl.ds(pl.multiple_of(pair * 128, 128), 128)
        q = q2[:, lanes]
        k = k2[:, lanes]
        v = v2[:, lanes]
        do = t3[:, lanes]
        prod = (f32(do) * f32(c2[:, lanes])).T
        kt = k.T
        parts = []
        dk = dv = None
        for e in range(2):
            h = pair * 2 + e
            p = p2[h]
            dom = pick(do, e)
            delta = jnp.sum(prod[e * 64 : (e + 1) * 64], axis=0, keepdims=True)
            dv_e = dot_nn(half(p), dom)
            ds = half(p * (dot_nt(v, dom) - delta))
            dk_e = dot_nn(ds, pick(q, e))
            parts.append(dot_nn(kt[e * 64 : (e + 1) * 64, :], ds))
            dk = dk_e if dk is None else dk + dk_e
            dv = dv_e if dv is None else dv + dv_e
        dk2s[:, lanes] = half(dk)
        dv2s[:, lanes] = half(dv)
        dqs[:, lanes] = half(jnp.concatenate(parts, axis=0).T)
        return carry

    lax.fori_loop(0, PAIRS, cross_backward, 0)
    weight_grad(n2, dqs, "cq")
    weight_grad(enc, dk2s, "ck")
    weight_grad(enc, dv2s, "cv")
    ck, cv, cq = weight("ck"), weight("cv"), weight("cq")

    def enc_body(at):
        g_enc[:, at] = dot_nt(dk2s[...], ck[at, :]) + dot_nt(dv2s[...], cv[at, :])

    cols_loop(D, enc_body)

    def n2_body(at):
        dn_acc[:, at] = dot_nt(dqs[...], cq[at, :])

    cols_loop(D, n2_body)
    rms_back(t2, t1, y1, dn_acc, 1)

    to_half_rows(cb, t2)
    weight_grad(c1, cb, "wo")
    back_project(t3, cb, "wo")

    def self_backward(pair, carry):
        lanes = pl.ds(pl.multiple_of(pair * 128, 128), 128)
        k = k1[:, lanes]
        v = v1[:, lanes]
        kt = k.T
        diags = [[None] * 3, [None] * 3]
        for i in (2, 1, 0):
            n = (i + 1) * 128
            at = slice(i * 128, (i + 1) * 128)
            do = t3[at, lanes]
            q = q1[at, lanes]
            prod = (f32(do) * f32(c1[at, lanes])).T
            parts = []
            dk = dv = None
            for e in range(2):
                h = pair * 2 + e
                p = p1[h, SELF_AT[i] : SELF_AT[i] + n, :]
                dom = pick(do, e)
                delta = jnp.sum(prod[e * 64 : (e + 1) * 64], axis=0, keepdims=True)
                dv_e = dot_nn(half(p), dom)
                ds = p * (dot_nt(v[:n], dom) - delta)
                for j in range(i + 1):
                    piece = ds[j * 128 : (j + 1) * 128]
                    was = diags[e][i - j]
                    diags[e][i - j] = piece if was is None else was + piece
                w = half(ds)
                dk_e = dot_nn(w, pick(q, e))
                parts.append(dot_nn(kt[e * 64 : (e + 1) * 64, :n], w))
                dk = dk_e if dk is None else dk + dk_e
                dv = dv_e if dv is None else dv + dv_e
            if i == 2:
                acc_k[...] = dk
                acc_v[...] = dv
            else:
                acc_k[:n] += dk
                acc_v[:n] += dv
            dqs[at, lanes] = half(jnp.concatenate(parts, axis=0).T)
        dks[:, lanes] = half(acc_k[...])
        dvs[:, lanes] = half(acc_v[...])
        for e in range(2):
            sums = []
            for delta in range(3):
                block = diags[e][delta]
                wide = jnp.concatenate([jnp.zeros_like(block), block], axis=1)
                total = wide[0:8]
                for a in range(1, 16):
                    total = total + pltpu.roll(wide[a * 8 : a * 8 + 8], 256 - 8 * a, 1)
                sums.append(jnp.sum(lane_roll_rows(total, -1), axis=0, keepdims=True))
            zero = jnp.zeros((1, 128), jnp.float32)
            diag[pl.ds(pair * 2 + e, 1), :] = (
                jnp.concatenate([sums[0], zero, zero, zero], axis=1)
                + jnp.concatenate([zero, sums[1], zero, zero], axis=1)
                + jnp.concatenate([zero, zero, sums[2], zero], axis=1)
            )
        return carry

    diag[...] = jnp.zeros_like(diag)
    lax.fori_loop(0, PAIRS, self_backward, 0)
    weight_grad(n1, dqs, "wq")
    weight_grad(n1, dks, "wk")
    weight_grad(n1, dvs, "wv")
    rest = diag[...]
    total = jnp.zeros((16, BUCKETS), jnp.float32)
    for _ in range(3):
        top = half(rest)
        total = total + dot_nt(top, one_hot)
        rest = rest - f32(top)
    g_table[...] = total
    wq, wk, wv = weight("wq"), weight("wk"), weight("wv")

    def n1_body(at):
        dn_acc[:, at] = dot_nt(dqs[...], wq[at, :]) + dot_nt(dks[...], wk[at, :]) + dot_nt(dvs[...], wv[at, :])

    cols_loop(D, n1_body)
    rms_back(g_in, t2, x, dn_acc, 0)
    for slot in range(3):
        pltpu.make_async_copy(stage.at[slot], g_wt.at[pl.ds(0, CH)], s_sem.at[slot]).wait()


def layer(x, enc, cot, gains, table, seg, eseg, full_sc, full_wt):
    vmem = pl.BlockSpec(memory_space=pltpu.VMEM)
    hbm = pl.BlockSpec(memory_space=pl.ANY)
    bf, fl = jnp.bfloat16, jnp.float32
    wide = lambda kind: pltpu.VMEM((ROWS, D), kind)
    thin = lambda kind: pltpu.VMEM((KEYS, D), kind)
    return pl.pallas_call(
        layer_kernel,
        out_shape=(
            jax.ShapeDtypeStruct((ROWS, D), fl),
            jax.ShapeDtypeStruct((ROWS, D), fl),
            jax.ShapeDtypeStruct((KEYS, D), fl),
            jax.ShapeDtypeStruct((3072, D), bf),
            jax.ShapeDtypeStruct((9216, D), bf),
            jax.ShapeDtypeStruct((3, D), fl),
            jax.ShapeDtypeStruct((16, BUCKETS), fl),
        ),
        in_specs=[vmem] * 7 + [hbm] * 2,
        out_specs=(vmem, vmem, vmem, hbm, hbm, vmem, vmem),
        scratch_shapes=[
            pltpu.VMEM((3072, D), bf),
            pltpu.VMEM((9216, D), bf),
            pltpu.VMEM((H, 3, 128, 128), fl),
            pltpu.VMEM((ROWS, ROWS), fl),
            pltpu.VMEM((KEYS, ROWS), fl),
            pltpu.VMEM((H, 768, 128), fl),
            pltpu.VMEM((H, KEYS, ROWS), fl),
            wide(bf), wide(bf), wide(bf), wide(bf), wide(bf), wide(fl),
            wide(bf), wide(bf), thin(bf), thin(bf), wide(bf), wide(fl), wide(bf), wide(bf),
            wide(fl), wide(fl), wide(bf),
            wide(bf), wide(bf), wide(bf), thin(bf), thin(bf), wide(fl),
            pltpu.VMEM((ROWS, 128), fl), pltpu.VMEM((ROWS, 128), fl),
            pltpu.VMEM((16, SPAN), fl),
            pltpu.VMEM((ROWS, CH), bf), pltpu.VMEM((ROWS, CH), bf), pltpu.VMEM((ROWS, CH), bf),
            pltpu.VMEM((3, CH, D), bf),
            pltpu.SemaphoreType.DMA((len(BLOCKS),)),
            pltpu.SemaphoreType.DMA((3,)),
        ],
        compiler_params=pltpu.CompilerParams(vmem_limit_bytes=62 << 20),
        name="layer",
    )(x, enc, cot, gains, table, seg, eseg, full_sc, full_wt)


def per_device(inputs, encoded, cotangent, scoring, weights, small_params, dec_segments, enc_segments):
    full_sc, full_wt, full_small = gather_params(scoring, weights, small_params)
    gains = full_small[: 3 * D].astype(jnp.float32).reshape(3, D)
    table = jnp.pad(full_small[3 * D :].reshape(BUCKETS, H).T, ((0, 4), (0, 0)))
    out, g_in, g_enc, g_sc, g_wt, g_gain, g_table = layer(
        inputs, encoded, cotangent, gains, table, dec_segments, enc_segments, full_sc, full_wt
    )
    g_small = jnp.concatenate([g_gain.reshape(-1), g_table[:H].T.reshape(-1)])
    o_sc, o_wt, o_sm = scatter_grads(g_sc, g_wt, g_small)
    return out, g_in, g_enc, o_sc, o_wt, o_sm


def solution(mesh):
    rows = P(("dp", "fsdp"), None)
    flat = P(("dp", "fsdp"))
    return jax.shard_map(
        per_device,
        mesh=mesh,
        in_specs=(rows, rows, rows, rows, rows, flat, rows, rows),
        out_specs=(rows, rows, rows, rows, rows, flat),
        check_vma=False,
    )
```

time: 991 us -> 234 us (0.24)
  waiting for transfers between devices: 423 us -> 0 us
  matrix products: 232 us -> 0 us
  Pallas kernels: 0 us -> 222 us
  blocking collectives: 198 us -> 0 us
  local copies, waits for them, and re-layouts: 62.4 us -> 10.7 us
  other arithmetic: 49.3 us -> 0.02 us
  between operations: 15.5 us -> 0.69 us
    reduce_scatter x2 -> x0, waiting for transfers between devices: 371 us -> none  [the longest x1 261 us: per_device(): lax.psum_scatter(weight_terms, ('dp', 'fsdp'), scatter_dimension=0, tiled...]
    dot_general x78 -> x0, matrix products: 232 us -> none  [the longest x12 66.1 us: block_scores(): jnp.einsum('khd,qhd->hkq', key_block, query_heads, preferred_element_type...]
    pallas_call x0 -> x3, Pallas kernels: none -> 222 us  [the longest x1 85.1 us: layer(): pl.pallas_call(layer_kernel, out_shape=(jax.ShapeDtypeStruct((ROWS, D), f...]
    unnamed x3 -> x0, blocking collectives: 198 us -> none
    all_gather x4 -> x0, waiting for transfers between devices: 49.4 us -> none  [the longest x1 25.1 us: per_device(): lax.all_gather(scoring_again, ('dp', 'fsdp'), axis=0, tiled=True)]
    and x9 -> x0, other arithmetic: 18.4 us -> none  [block_scores(): allowed = allowed & (distance >= 0)]
    unnamed x141 -> x3, local copies, waits for them, and re-layouts: 17.8 us -> 3.23 us
  transfers between devices with their start and end apart: 6 -> 0, of which waited for: 5 -> 0; matrix products, arithmetic and copies ran while one was open for 14% -> 0% of each run, Pallas kernels for 0% -> 0%
where the time goes in v1:
time: 234 us; the launch traced here: 233 us
  Pallas kernels  222 us (95%)
  local copies, waits for them, and re-layouts  10.7 us (5%)
    pallas_call x1, Pallas kernels, layer(): pl.pallas_call(layer_kernel, out_shape=(jax.ShapeDtypeStruct((ROWS, D), f...  85.1 us
    pallas_call x1, Pallas kernels, scatter_grads(): pl.pallas_call(scatter_kernel, out_shape=(jax.ShapeDtypeStruct((SC_ROWS,...  79.5 us
    pallas_call x1, Pallas kernels, gather_params(): pl.pallas_call(gather_kernel, out_shape=(jax.ShapeDtypeStruct((4, 4, 4, 2...  57.3 us

profile of v1, /device:TPU:0, one launch (start us, length us, event | category | flops | bytes accessed | tf_op | source)
XLA Modules:
  0.0 233.3 jit_solution(16106885113460968445)
XLA Ops:
  0.6 1.2 pad.12.sm_in
  1.9 57.3 %gather_params.1 = (bf16[4,4,4,2,24,768]{5,4,3,2,1,0:T(8,128)(2,1)}, bf16[4,4,4,2,72,768]{5,4,3,2,1,0:T(8,128)(2,1)}, bf16[4,4,4,2,8,128]{5,4,3,2,1,0:T(8,128)(2,1)}) custom-call(bf16[24,768]{1,0:T(8,128)(2,1)} %sc_in.1, bf16[72,768]{1,0:T(8,128)(2,1)} %wt_in.1, bf16[8,128]{1,0:T(8,128)(2,1)} %pad.12.sm_in), custom_call_target="tpu_custom_call" | custom-call | tf_op jit(solution)/shard_map/gather_params/pallas_call | solution.py:137
  59.2 1.2 slice_reduce_fusion
  60.3 0.1 slice.17
  60.5 0.1 copy.16
  60.5 0.6 pad.13.table
  61.2 0.2 reshape_squeeze.3
  61.4 0.6 reshape.55.gains
  62.0 85.1 %layer.1 = (f32[384,768]{1,0:T(8,128)}, f32[384,768]{1,0:T(8,128)}, f32[192,768]{1,0:T(8,128)}, bf16[3072,768]{1,0:T(8,128)(2,1)}, bf16[9216,768]{1,0:T(8,128)(2...) custom-call(f32[384,768]{1,0:T(8,128)} %x.7, bf16[192,768]{1,0:T(8,128)(2,1)} %enc.1, f32[384,768]{1,0:T(8,128)} %cot.1, ...), custom_call_target="tpu_custom_call" | custom-call | tf_op jit(solution)/shard_map/layer/pallas_call | solution.py:819
  147.1 0.7 slice_bitcast_fusion
  147.8 0.1 copy.15
  147.9 0.1 reshape.52
  148.0 0.7 reshape.51
  148.8 0.6 pad.14.g_sm
  149.4 79.5 %scatter_grads.1 = (f32[24,768]{1,0:T(8,128)}, f32[72,768]{1,0:T(8,128)}, f32[24,128]{1,0:T(8,128)}) custom-call(bf16[4,4,4,2,24,768]{5,4,3,2,1,0:T(8,128)(2,1)} %bitcast.14, bf16[4,4,4,2,72,768]{5,4,3,2,1,0:T(8,128)(2,1)} %bitcast.11, f32[24,128]{1,0:T(8,128)} %pad.14.g_sm), custom_call_target="tpu_custom_call" | custom-call | tf_op jit(solution)/shard_map/scatter_grads/pallas_call | solution.py:355
  228.9 1.3 dynamic_slice.3
  230.2 1.5 copy.19
  231.7 1.6 copy.20
  (3 shorter events, 0.0 us)
